TPU v7x, 32 devices: a whole 2x2x4 slice. The times are simulated.
32 devices in a mesh: groups: 2 (over y), seq: 4 (over z), cell: 4 (over x, core).
Axes of the slice: x: 2, y: 2, z: 4, core: 2. Of those that a mesh axis runs over, the one named last changes fastest.
Arguments:
- dna_bases: int32 [65536], P(('groups', 'seq')), parts along dimension 0, may hold values from 0 to 3
- stem_weight: bfloat16 [512, 768], replicated, may hold values from -0.5 to 0.5
- conv_weight: bfloat16 [2, 384, 3, 768], P(None, 'cell'), may hold values from -0.125 to 0.125
- proj_weight: bfloat16 [2, 384, 768], P(None, 'cell'), may hold values from -0.3125 to 0.3125
- emission_head_weight: bfloat16 [32, 768, 128], P('cell'), may hold values from -0.046875 to 0.046875
- transitions: float32 [32, 128, 128], P('cell'), may hold values from -1 to 109
Outputs:
- log_marginals: float32 [32, 512, 128], P('cell', ('groups', 'seq')), parts along dimension 1
There are 2 independent parts, one for each index of `groups`. A program takes and returns all parts, laid end to end along the dimension named above; an argument that names none is the same for every part. Nothing has to cross between parts.
All inputs are finite; a program needn't handle non-finite values.
Results may differ from a plain program's by a relative error of at most 0.0007.
Values may be sent and summed in bfloat16 or wider, within the bound.
A program may use at most 128 MiB of HBM per device.

v0:
```python
import jax
import jax.numpy as jnp
from jax import lax
from jax.sharding import PartitionSpec as P

BIN_BP = 128
BASE_DILATION = 4


def with_halo(block, sides, width):
    for axis, dim in sides:
        count = lax.axis_size(axis)
        forward = [(i, i + 1) for i in range(count - 1)]
        backward = [(target, source) for source, target in forward]
        low = lax.ppermute(
            lax.slice_in_dim(block, block.shape[dim] - width, None, axis=dim), axis, forward
        )
        high = lax.ppermute(lax.slice_in_dim(block, 0, width, axis=dim), axis, backward)
        block = jnp.concatenate([low, block, high], axis=dim)
    return block


def prefix(value, axis, join, neutral, backward):
    count = lax.axis_size(axis)
    place = lax.axis_index(axis)
    ahead = count - 1 - place if backward else place
    gathered = lax.all_gather(value.astype(jnp.bfloat16), axis)
    state = jnp.zeros_like(value) + jnp.asarray(neutral, value.dtype)

    def one(lap, state):
        source = count - 1 - lap if backward else lap
        return join(state, lax.dynamic_index_in_dim(gathered, source, 0, False).astype(value.dtype))

    return lax.fori_loop(0, ahead, one, state)


def scaled(values):
    return values * lax.rsqrt(jnp.mean(values * values, axis=-1, keepdims=True) + 1e-06)


def tap_stack(conv_input, spacing_multiplier):
    out_rows = conv_input.shape[0] - 2 * spacing_multiplier
    return jnp.concatenate(
        [
            conv_input[0:out_rows],
            conv_input[spacing_multiplier : spacing_multiplier + out_rows],
            conv_input[2 * spacing_multiplier : 2 * spacing_multiplier + out_rows],
        ],
        axis=1,
    )


def mat_prod(left_mat, trailing_product):
    return jnp.einsum("crs,cst->crt", left_mat, trailing_product, precision=lax.Precision.HIGHEST)


def unit_peak(matrix):
    return matrix / jnp.max(matrix, axis=(-2, -1), keepdims=True)


def vec_peak(vector):
    return vector / jnp.max(vector, axis=-1, keepdims=True)


def forward_join(early_mat, late_mat):
    return unit_peak(mat_prod(early_mat, late_mat))


def backward_join(early_mat, late_mat):
    return unit_peak(mat_prod(late_mat, early_mat))


def branch(stacked, conv_slice, proj_slice):
    flat_weight = conv_slice.reshape(conv_slice.shape[0], -1)
    conv_out = lax.dot_general(
        stacked, flat_weight, (((1,), (1,)), ((), ())), preferred_element_type=jnp.float32
    )
    hidden = jax.nn.gelu(conv_out).astype(jnp.bfloat16)
    partial_value = jnp.dot(hidden, proj_slice, preferred_element_type=jnp.float32)
    return lax.psum(partial_value.astype(jnp.bfloat16), "cell").astype(jnp.float32)


def per_device(dna_bases, stem_weight, conv_weight, proj_weight, emission_head_weight, transitions):
    bin_rows = dna_bases.shape[0] // BIN_BP
    base_hits = dna_bases.reshape(bin_rows, BIN_BP, 1) == jnp.arange(4, dtype=jnp.int32)
    one_hot = base_hits.astype(jnp.bfloat16).reshape(bin_rows, BIN_BP * 4)
    stem_out = jnp.dot(one_hot, stem_weight, preferred_element_type=jnp.float32).astype(
        jnp.bfloat16
    )
    layers = conv_weight.shape[0]
    residual = stem_out.astype(jnp.float32)
    for layer_position in range(layers):
        spacing_multiplier = BASE_DILATION * 2**layer_position
        conv_input = jax.nn.gelu(scaled(residual)).astype(jnp.bfloat16)
        widened = with_halo(conv_input, (("seq", 0),), spacing_multiplier)
        residual = residual + branch(
            tap_stack(widened, spacing_multiplier),
            conv_weight[layer_position],
            proj_weight[layer_position],
        )
    trunk_features = scaled(residual).astype(jnp.bfloat16)
    emission_scores = jnp.einsum(
        "td,cds->cts", trunk_features, emission_head_weight, preferred_element_type=jnp.float32
    )
    cell_count = emission_scores.shape[0]
    state_count = emission_scores.shape[2]
    scaling = jnp.exp(emission_scores - jnp.max(emission_scores, axis=2, keepdims=True))
    trans_exp = jnp.exp(transitions - jnp.max(transitions, axis=(1, 2), keepdims=True))
    sub_len = 8
    sub_count = bin_rows // sub_len
    factors = scaling.reshape(cell_count, sub_count, sub_len, state_count)

    def block_product(inputs):
        transition_matrix, factor = inputs
        running_state = transition_matrix[None] * factor[:, 0, None, :]
        for position in range(1, sub_len):
            running_state = (
                jnp.einsum(
                    "ylv,vu->ylu", running_state, transition_matrix, precision=lax.Precision.HIGHEST
                )
                * factor[:, position, None, :]
            )
            running_state = unit_peak(running_state)
        combined = running_state
        for level_index in range(sub_count.bit_length() - 1):
            half_count = combined.shape[0] // 2
            paired_states = combined.reshape(half_count, 2, state_count, state_count)
            combined = unit_peak(
                jnp.einsum(
                    "mpw,mwy->mpy",
                    paired_states[:, 0],
                    paired_states[:, 1],
                    precision=lax.Precision.HIGHEST,
                )
            )
        return (running_state, combined[0])

    segment_list, block = lax.map(block_product, (trans_exp, factors))
    identity = jnp.broadcast_to(jnp.eye(state_count, dtype=jnp.float32), block.shape)
    prefix_mat = prefix(block, "seq", forward_join, identity, False)
    suffix_mat = prefix(block, "seq", backward_join, identity, True)
    enter_vec = vec_peak(jnp.sum(prefix_mat, axis=1))
    leave_vec = vec_peak(jnp.sum(suffix_mat, axis=2))
    chain_pieces = jnp.swapaxes(segment_list, 0, 1)

    def forward_step(vector, piece_mat):
        return (
            vec_peak(jnp.einsum("cr,crs->cs", vector, piece_mat, precision=lax.Precision.HIGHEST)),
            vector,
        )

    def backward_step(vector, piece_mat):
        return (
            vec_peak(jnp.einsum("crs,cs->cr", piece_mat, vector, precision=lax.Precision.HIGHEST)),
            vector,
        )

    _, starts = lax.scan(forward_step, enter_vec, chain_pieces)
    _, after_vecs = lax.scan(backward_step, leave_vec, chain_pieces, reverse=True)
    vector = jnp.swapaxes(starts, 0, 1)
    forward_list = []
    for position in range(sub_len):
        vector = vec_peak(
            jnp.einsum("cgr,crs->cgs", vector, trans_exp, precision=lax.Precision.HIGHEST)
            * factors[:, :, position]
        )
        forward_list.append(vector)
    vector = jnp.swapaxes(after_vecs, 0, 1)
    backward_list = [vector] * sub_len
    for position in range(sub_len - 1, -1, -1):
        backward_list[position] = vector
        if position > 0:
            vector = vec_peak(
                jnp.einsum(
                    "crs,cgs->cgr",
                    trans_exp,
                    factors[:, :, position] * vector,
                    precision=lax.Precision.HIGHEST,
                )
            )
    alpha_all = jnp.stack(forward_list, axis=2).reshape(cell_count, bin_rows, state_count)
    beta_all = jnp.stack(backward_list, axis=2).reshape(cell_count, bin_rows, state_count)
    joint_log = jnp.log(alpha_all) + jnp.log(beta_all)
    return jnp.maximum(joint_log - jax.nn.logsumexp(joint_log, axis=2, keepdims=True), -30.0)


def solution(mesh):
    placed = (
        P(("groups", "seq")),
        P(),
        P(None, "cell", None, None),
        P(None, "cell", None),
        P("cell", None, None),
        P("cell", None, None),
    )
    return jax.shard_map(
        per_device,
        mesh=mesh,
        in_specs=placed,
        out_specs=P("cell", ("groups", "seq"), None),
        check_vma=False,
    )
```

profile of v0, /device:TPU:0, one launch (start us, length us, event | category | flops | bytes accessed | tf_op | source)
XLA Modules:
  0.0 269.2 jit_solution(5592147471232159884)
XLA Ops:
  6.5 1.0 copy.102
  7.7 1.7 multiply_reduce_fusion.2
  9.5 5.0 %collective-permute-start = (bf16[4,768]{1,0:T(4,128)(2,1)S(1)}, bf16[4,768]{1,0:T(4,128)(2,1)S(1)}, u32[]{:S(2)}, u32[]{:S(2)}) collective-permute-start(bf16[4,768]{1,0:T(4,128)(2,1)S(1)} %get-tuple-element.359), channel_id=1, source_target_pairs={{0,4},{4,8},{8,12},{1,5},{5,9},{9,13},{2,6},{6,10},{10,14},{3,7},{... | collective-permute-start | bytes 18440 | tf_op jit(solution)/shard_map/ppermute | solution.py:15
  14.5 1.4 collective-permute-start.1
  16.0 1.2 fusion.211
  17.6 2.6 collective-permute-done.1
  20.2 2.0 convolution_convert_fusion.2
  22.3 32.0 %all-reduce.3.cloned.1.call-done = bf16[64,768]{1,0:T(8,128)(2,1)} async-done(((bf16[64,768]{1,0:T(8,128)(2,1)}), bf16[64,768]{1,0:T(8,128)(2,1)}) %all-reduce.3.cloned.1.call-update) | async-done | bytes 98320 | tf_op jit(solution)/shard_map/psum | solution.py:80
  54.3 1.1 multiply_reduce_fusion.1
  55.4 1.0 fusion.111
  56.5 3.4 %collective-permute-start.2 = (bf16[8,768]{1,0:T(8,128)(2,1)S(1)}, bf16[8,768]{1,0:T(8,128)(2,1)S(1)}, u32[]{:S(2)}, u32[]{:S(2)}) collective-permute-start(bf16[8,768]{1,0:T(8,128)(2,1)S(1)} %get-tuple-element.357), channel_id=1, source_target_pairs={{0,4},{4,8},{8,12},{1,5},{5,9},{9,13},{2,6},{6,10},{10,14},{3,7},{... | collective-permute-start | bytes 36872 | tf_op jit(solution)/shard_map/ppermute | solution.py:15
  59.9 1.3 collective-permute-start.3
  61.8 3.7 %collective-permute-done.3 = bf16[8,768]{1,0:T(8,128)(2,1)S(1)} collective-permute-done((bf16[8,768]{1,0:T(8,128)(2,1)S(1)}, bf16[8,768]{1,0:T(8,128)(2,1)S(1)}, u32[]{:S(2)}, u32[]{:S(2)}) %collective-permute-start.3) | collective-permute-done | bytes 12320 | tf_op jit(solution)/shard_map/ppermute | solution.py:18
  65.5 2.0 convolution_convert_fusion.1
  67.7 30.7 %all-reduce.5.cloned.1.call-done = bf16[64,768]{1,0:T(8,128)(2,1)} async-done(((bf16[64,768]{1,0:T(8,128)(2,1)}), bf16[64,768]{1,0:T(8,128)(2,1)}) %all-reduce.5.cloned.1.call-update) | async-done | bytes 98320 | tf_op jit(solution)/shard_map/psum | solution.py:80
  98.4 1.0 multiply_reduce_fusion
  99.5 1.4 fusion.66
  100.9 73.1 %while.62 = (s32[]{:T(128)}, f32[8,8,128,128]{3,2,0,1:T(8,128)}, bf16[8,128,128]{2,1,0:T(8,128)(2,1)}, f32[8,128,128]{2,1,0:T(8,128)S(1)}, f32[8,8,8,128]{3,2,1,0:T(8,128)S(1)}, /*index=5*/s32[]{:T(128)}) while((s32[]{:T(128)}, f32[8,8,128,128]{3,2,0,1:T(8,128)}, bf16[8,128,128]{2,1,0:T(8,128)(2,1)}, f32[8,128,128]{2,1,0:T(8,128)S(1)}, ...), condition=%wide.region_18.19_spmd, body=%wide.region_7.18_spmd.sunk | while | flops 1588559872 | bytes 11572125 | solution.py:138
  106.0 1.0 bitcast_dynamic-update-slice_fusion.6
  108.8 1.2 bitcast_dynamic-update-slice_fusion.7
  115.1 0.9 bitcast_dynamic-update-slice_fusion.6
  117.9 1.2 bitcast_dynamic-update-slice_fusion.7
  124.3 1.0 bitcast_dynamic-update-slice_fusion.6
  127.1 1.2 bitcast_dynamic-update-slice_fusion.7
  133.4 1.0 bitcast_dynamic-update-slice_fusion.6
  136.2 1.2 bitcast_dynamic-update-slice_fusion.7
  142.5 1.0 bitcast_dynamic-update-slice_fusion.6
  145.3 1.2 bitcast_dynamic-update-slice_fusion.7
  151.6 1.0 bitcast_dynamic-update-slice_fusion.6
  154.5 1.2 bitcast_dynamic-update-slice_fusion.7
  160.8 1.0 bitcast_dynamic-update-slice_fusion.6
  163.6 1.2 bitcast_dynamic-update-slice_fusion.7
  169.9 1.0 bitcast_dynamic-update-slice_fusion.6
  172.7 1.2 bitcast_dynamic-update-slice_fusion.7
  174.3 27.8 %all-gather.3.cloned.1.call-done = bf16[32,128,128]{2,1,0:T(8,128)(2,1)} async-done(((bf16[8,128,128]{2,1,0:T(8,128)(2,1)}), bf16[32,128,128]{2,1,0:T(8,128)(2,1)}) %all-gather.3.cloned.1.call-update) | async-done | bytes 1048592 | tf_op jit(solution)/shard_map/all_gather | solution.py:27
  202.6 14.4 %while.64 = (s32[]{:T(128)}, f32[8,128]{1,0:T(8,128)S(1)}, f32[8,8,128]{2,1,0:T(8,128)S(1)}, f32[8,8,128,128]{3,2,1,0:T(8,128)}, s32[]{:T(128)}, /*index=5*/f32[]{:T(128)}) while((s32[]{:T(128)}, f32[8,128]{1,0:T(8,128)S(1)}, f32[8,8,128]{2,1,0:T(8,128)S(1)}, f32[8,8,128,128]{3,2,1,0:T(8,128)}, s32[]{:T(128)}, /*index=5*/f32[]{:T(128)}) %tuple.192), condition=%wide.region_26.27_spmd, body=%wide.region_24.26_spmd.sunk | while | flops 1574906 | bytes 553613 | solution.py:158
  202.6 1.6 fusion.296
  204.4 1.6 fusion.296
  206.2 1.6 fusion.296
  208.0 1.6 fusion.296
  209.8 1.6 fusion.296
  211.6 1.6 fusion.296
  213.4 1.6 fusion.296
  215.2 1.6 fusion.296
  218.3 5.0 %while.65 = (s32[]{:T(128)}, f32[8,128,128]{2,1,0:T(8,128)S(1)}, s32[]{:T(128)}, bf16[4,8,128,128]{3,2,1,0:T(8,128)(2,1)}, s32[]{:T(128)}, /*index=5*/s32[]{:T(128)}, s32[]{:T(128)}, s32[]{:T(128)}) while((s32[]{:T(128)}, f32[8,128,128]{2,1,0:T(8,128)S(1)}, s32[]{:T(128)}, bf16[4,8,128,128]{3,2,1,0:T(8,128)(2,1)}, s32[]{:T(128)}, ...), condition=%wide.region_37.38_spmd, body=%wide.region_35.37_spmd.sunk | while | flops 201588736 | bytes 2359495 | solution.py:34
  218.3 1.4 fusion.298
  219.9 1.4 fusion.298
  221.5 1.4 fusion.298
  223.7 17.6 %while.66 = (s32[]{:T(128)}, f32[8,128]{1,0:T(8,128)S(1)}, f32[8,8,128]{2,0,1:T(8,128)S(1)}, f32[8,8,128,128]{3,2,1,0:T(8,128)}, s32[]{:T(128)}, /*index=5*/s32[]{:T(128)}, f32[]{:T(128)}, s32[]{:T(128)}) while((s32[]{:T(128)}, f32[8,128]{1,0:T(8,128)S(1)}, f32[8,8,128]{2,0,1:T(8,128)S(1)}, f32[8,8,128,128]{3,2,1,0:T(8,128)}, s32[]{:T(128)}, ...), condition=%wide.region_42.43_spmd, body=%wide.region_40.42_spmd.sunk | while | flops 1574907 | bytes 553133 | solution.py:159
  223.7 2.0 fusion.301
  225.9 2.0 fusion.301
  228.1 2.0 fusion.301
  230.3 2.0 fusion.301
  232.5 2.0 fusion.301
  234.7 2.0 fusion.301
  236.9 2.0 fusion.301
  239.1 2.0 fusion.301
  249.0 0.9 fusion.149
  250.5 1.0 fusion.161
  252.1 1.0 fusion.159
  253.7 1.0 fusion.157
  255.3 1.0 fusion.155
  256.9 1.0 fusion.153
  258.5 1.0 fusion.151
  (264 shorter events, 77.3 us)
Async XLA Ops:
  6.5 92.9 %copy-start = (bf16[8,768,128]{2,1,0:T(8,128)(2,1)S(1)}, bf16[8,768,128]{2,1,0:T(8,128)(2,1)}, u32[]{:S(2)}) copy-start(bf16[8,768,128]{2,1,0:T(8,128)(2,1)} %param.20) | copy-start | bytes 4718596
  6.5 47.8 %all-reduce.3.cloned.1.call-start = ((), (), s32[]{:S(2)}) async-start(), calls=%async_computation | async-start | bytes 196608 | tf_op jit(solution)/shard_map/psum | solution.py:80
  9.5 8.1 %collective-permute-start = (bf16[4,768]{1,0:T(4,128)(2,1)S(1)}, bf16[4,768]{1,0:T(4,128)(2,1)S(1)}, u32[]{:S(2)}, u32[]{:S(2)}) collective-permute-start(bf16[4,768]{1,0:T(4,128)(2,1)S(1)} %get-tuple-element.359), channel_id=1, source_target_pairs={{0,4},{4,8},{8,12},{1,5},{5,9},{9,13},{2,6},{6,10},{10,14},{3,7},{... | collective-permute-start | bytes 18440 | tf_op jit(solution)/shard_map/ppermute | solution.py:15
  14.5 47.1 %copy-start.1 = (f32[8,128,128]{2,1,0:T(8,128)S(1)}, f32[8,128,128]{2,1,0:T(8,128)}, u32[]{:S(2)}) copy-start(f32[8,128,128]{2,1,0:T(8,128)} %param.21) | copy-start | bytes 1572868
  14.5 5.7 %collective-permute-start.1 = (bf16[4,768]{1,0:T(4,128)(2,1)S(1)}, bf16[4,768]{1,0:T(4,128)(2,1)S(1)}, u32[]{:S(2)}, u32[]{:S(2)}) collective-permute-start(bf16[4,768]{1,0:T(4,128)(2,1)S(1)} %get-tuple-element.360), channel_id=1, source_target_pairs={{4,0},{8,4},{12,8},{5,1},{9,5},{13,9},{6,2},{10,6},{14,10},{7,3},{... | collective-permute-start | bytes 18440 | tf_op jit(solution)/shard_map/ppermute | solution.py:18
  22.2 76.2 %all-reduce.5.cloned.1.call-start = ((), (), s32[]{:S(2)}) async-start(), calls=%async_computation.1 | async-start | bytes 196608 | tf_op jit(solution)/shard_map/psum | solution.py:80
  54.3 44.1 %copy-start.2 = (bf16[64,768]{1,0:T(8,128)(2,1)S(1)}, bf16[64,768]{1,0:T(8,128)(2,1)}, u32[]{:S(2)}) copy-start(bf16[64,768]{1,0:T(8,128)(2,1)} %all-reduce.3.cloned.1.call-done) | copy-start | bytes 294916
  56.5 5.3 %collective-permute-start.2 = (bf16[8,768]{1,0:T(8,128)(2,1)S(1)}, bf16[8,768]{1,0:T(8,128)(2,1)S(1)}, u32[]{:S(2)}, u32[]{:S(2)}) collective-permute-start(bf16[8,768]{1,0:T(8,128)(2,1)S(1)} %get-tuple-element.357), channel_id=1, source_target_pairs={{0,4},{4,8},{8,12},{1,5},{5,9},{9,13},{2,6},{6,10},{10,14},{3,7},{... | collective-permute-start | bytes 36872 | tf_op jit(solution)/shard_map/ppermute | solution.py:15
  59.9 5.6 %collective-permute-start.3 = (bf16[8,768]{1,0:T(8,128)(2,1)S(1)}, bf16[8,768]{1,0:T(8,128)(2,1)S(1)}, u32[]{:S(2)}, u32[]{:S(2)}) collective-permute-start(bf16[8,768]{1,0:T(8,128)(2,1)S(1)} %get-tuple-element.358), channel_id=1, source_target_pairs={{4,0},{8,4},{12,8},{5,1},{9,5},{13,9},{6,2},{10,6},{14,10},{7,3},{... | collective-permute-start | bytes 36872 | tf_op jit(solution)/shard_map/ppermute | solution.py:18
  67.5 134.7 %all-gather.3.cloned.1.call-start = ((), (), s32[]{:S(2)}) async-start(), calls=%async_computation.2 | async-start | bytes 1310720 | tf_op jit(solution)/shard_map/all_gather | solution.py:27
Sparse Core Ops, SparseCore 0:
  22.4 31.9 all-reduce.2
  67.6 30.7 all-reduce.4
  174.1 27.9 all-gather.2
where the time goes:
time: 271 us; the launch traced here: 269 us
  matrix products  104 us (38%)
  waiting for transfers between devices  96.8 us (36%)
  other arithmetic  37.8 us (14%)
  between operations  13.5 us (5%)
  starting transfers between devices  11.1 us (4%)
  local copies, waits for them, and re-layouts  4.66 us (2%)
    psum x2, waiting for transfers between devices, branch(): lax.psum(partial_value.astype(jnp.bfloat16), 'cell').astype(jnp.float32)  62.7 us
    dot_general x56, matrix products, block_product(): jnp.einsum('ylv,vu->ylu', running_state, transition_matrix, precision=lax...  40 us
    all_gather x1, waiting for transfers between devices, prefix(): gathered = lax.all_gather(value.astype(jnp.bfloat16), axis)  27.8 us
    dynamic_update_slice x16, other arithmetic, per_device(): segment_list, block = lax.map(block_product, (trans_exp, factors))  17.7 us
    dot_general x8, matrix products, backward_step(): jnp.einsum('crs,cs->cr', piece_mat, vector, precision=lax.Precision.HIGHEST)  15.7 us
    dot_general x24, matrix products, block_product(): jnp.einsum('mpw,mwy->mpy', paired_states[:, 0], paired_states[:, 1], prec...  13.3 us
    dot_general x8, matrix products, forward_step(): jnp.einsum('cr,crs->cs', vector, piece_mat, precision=lax.Precision.HIGHEST)  12.8 us
    div x33, other arithmetic, vec_peak(): return vector / jnp.max(vector, axis=-1, keepdims=True)  10.7 us
  transfers between devices with their start and end apart: 7, of which 5 were waited for; matrix products, arithmetic and copies ran while one was open for 1% of the time, Pallas kernels for 0%

commit v1 on v0

--- a/solution.py
+++ b/solution.py
@@ -77,7 +77,9 @@
     )
     hidden = jax.nn.gelu(conv_out).astype(jnp.bfloat16)
     partial_value = jnp.dot(hidden, proj_slice, preferred_element_type=jnp.float32)
-    return lax.psum(partial_value.astype(jnp.bfloat16), "cell").astype(jnp.float32)
+    return jnp.sum(lax.all_gather(partial_value.astype(jnp.bfloat16), "cell"), axis=0).astype(
+        jnp.float32
+    )
 
 
 def per_device(dna_bases, stem_weight, conv_weight, proj_weight, emission_head_weight, transitions):

time: 271 us -> 214 us (0.79)
  waiting for transfers between devices: 96.8 us -> 32.8 us
  blocking collectives: 0 us -> 12.6 us
    psum x2 -> x0, waiting for transfers between devices: 62.7 us -> none  [branch(): lax.psum(partial_value.astype(jnp.bfloat16), 'cell').astype(jnp.float32)]
    all_gather x0 -> x2, blocking collectives: none -> 12.6 us  [branch(): lax.all_gather(partial_value.astype(jnp.bfloat16), 'cell')]
  transfers between devices with their start and end apart: 7 -> 5, of which waited for: 5 -> 3; matrix products, arithmetic and copies ran while one was open for 1% -> 1% of each run, Pallas kernels for 0% -> 0%
where the time goes in v1:
time: 214 us; the launch traced here: 213 us
  matrix products  102 us (48%)
  other arithmetic  35.2 us (16%)
  waiting for transfers between devices  32.8 us (15%)
  between operations  13.8 us (6%)
  blocking collectives  12.6 us (6%)
  starting transfers between devices  11 us (5%)
  local copies, waits for them, and re-layouts  4.68 us (2%)
    dot_general x56, matrix products, block_product(): jnp.einsum('ylv,vu->ylu', running_state, transition_matrix, precision=lax...  40 us
    all_gather x1, waiting for transfers between devices, prefix(): gathered = lax.all_gather(value.astype(jnp.bfloat16), axis)  26.7 us
    dynamic_update_slice x16, other arithmetic, per_device(): segment_list, block = lax.map(block_product, (trans_exp, factors))  17.7 us
    dot_general x8, matrix products, backward_step(): jnp.einsum('crs,cs->cr', piece_mat, vector, precision=lax.Precision.HIGHEST)  15.7 us
    dot_general x24, matrix products, block_product(): jnp.einsum('mpw,mwy->mpy', paired_states[:, 0], paired_states[:, 1], prec...  13.3 us
    dot_general x8, matrix products, forward_step(): jnp.einsum('cr,crs->cs', vector, piece_mat, precision=lax.Precision.HIGHEST)  12.8 us
    all_gather x2, blocking collectives, branch(): lax.all_gather(partial_value.astype(jnp.bfloat16), 'cell')  12.6 us
    div x33, other arithmetic, vec_peak(): return vector / jnp.max(vector, axis=-1, keepdims=True)  10.7 us
  transfers between devices with their start and end apart: 5, of which 3 were waited for; matrix products, arithmetic and copies ran while one was open for 1% of the time, Pallas kernels for 0%

profile of v1, /device:TPU:0, one launch (start us, length us, event | category | flops | bytes accessed | tf_op | source)
XLA Modules:
  0.0 213.1 jit_solution(11532496796395993112)
XLA Ops:
  6.5 1.0 copy.102
  7.7 1.7 multiply_reduce_fusion.2
  9.6 5.0 %collective-permute-start = (bf16[4,768]{1,0:T(4,128)(2,1)S(1)}, bf16[4,768]{1,0:T(4,128)(2,1)S(1)}, u32[]{:S(2)}, u32[]{:S(2)}) collective-permute-start(bf16[4,768]{1,0:T(4,128)(2,1)S(1)} %get-tuple-element.359), channel_id=1, source_target_pairs={{0,4},{4,8},{8,12},{1,5},{5,9},{9,13},{2,6},{6,10},{10,14},{3,7},{... | collective-permute-start | bytes 18440 | tf_op jit(solution)/shard_map/ppermute | solution.py:15
  14.5 1.3 collective-permute-start.1
  15.8 1.2 fusion.211
  17.7 2.4 %collective-permute-done.1 = bf16[4,768]{1,0:T(4,128)(2,1)S(1)} collective-permute-done((bf16[4,768]{1,0:T(4,128)(2,1)S(1)}, bf16[4,768]{1,0:T(4,128)(2,1)S(1)}, u32[]{:S(2)}, u32[]{:S(2)}) %collective-permute-start.1) | collective-permute-done | bytes 6176 | tf_op jit(solution)/shard_map/ppermute | solution.py:18
  20.1 1.4 convolution_convert_fusion.2
  21.5 6.5 %all-gather = bf16[256,768]{1,0:T(8,128)(2,1)S(1)} all-gather(bf16[64,768]{1,0:T(8,128)(2,1)S(1)} %convolution_convert_fusion.2), channel_id=2, replica_groups=mesh['groups'=2,'seq'=4,'cell'=4] {'cell'}, dimensions={0}, use_global_device_ids=true | all-gather | bytes 491520 | tf_op jit(solution)/shard_map/all_gather | solution.py:80
  28.3 3.5 %collective-permute-start.2 = (bf16[8,768]{1,0:T(8,128)(2,1)S(1)}, bf16[8,768]{1,0:T(8,128)(2,1)S(1)}, u32[]{:S(2)}, u32[]{:S(2)}) collective-permute-start(bf16[8,768]{1,0:T(8,128)(2,1)S(1)} %get-tuple-element.357), channel_id=1, source_target_pairs={{0,4},{4,8},{8,12},{1,5},{5,9},{9,13},{2,6},{6,10},{10,14},{3,7},{... | collective-permute-start | bytes 36872 | tf_op jit(solution)/shard_map/ppermute | solution.py:15
  31.8 1.3 collective-permute-start.3
  33.7 3.7 %collective-permute-done.3 = bf16[8,768]{1,0:T(8,128)(2,1)S(1)} collective-permute-done((bf16[8,768]{1,0:T(8,128)(2,1)S(1)}, bf16[8,768]{1,0:T(8,128)(2,1)S(1)}, u32[]{:S(2)}, u32[]{:S(2)}) %collective-permute-start.3) | collective-permute-done | bytes 12320 | tf_op jit(solution)/shard_map/ppermute | solution.py:18
  37.4 1.4 convolution_convert_fusion.1
  38.7 6.1 %all-gather.1 = bf16[256,768]{1,0:T(8,128)(2,1)S(1)} all-gather(bf16[64,768]{1,0:T(8,128)(2,1)S(1)} %convolution_convert_fusion.1), channel_id=3, replica_groups=mesh['groups'=2,'seq'=4,'cell'=4] {'cell'}, dimensions={0}, use_global_device_ids=true | all-gather | bytes 491520 | tf_op jit(solution)/shard_map/all_gather | solution.py:80
  45.7 73.1 %while.62 = (s32[]{:T(128)}, f32[8,8,128,128]{3,2,0,1:T(8,128)}, bf16[8,128,128]{2,1,0:T(8,128)(2,1)}, f32[8,128,128]{2,1,0:T(8,128)S(1)}, f32[8,8,8,128]{3,2,1,0:T(8,128)S(1)}, /*index=5*/s32[]{:T(128)}) while((s32[]{:T(128)}, f32[8,8,128,128]{3,2,0,1:T(8,128)}, bf16[8,128,128]{2,1,0:T(8,128)(2,1)}, f32[8,128,128]{2,1,0:T(8,128)S(1)}, ...), condition=%wide.region_18.19_spmd, body=%wide.region_7.18_spmd.sunk | while | flops 1588559872 | bytes 11572125 | solution.py:140
  50.8 1.0 bitcast_dynamic-update-slice_fusion.6
  53.6 1.2 bitcast_dynamic-update-slice_fusion.7
  59.9 0.9 bitcast_dynamic-update-slice_fusion.6
  61.9 0.8 fusion.291
  62.7 1.2 bitcast_dynamic-update-slice_fusion.7
  69.0 1.0 bitcast_dynamic-update-slice_fusion.6
  71.0 0.8 fusion.291
  71.8 1.2 bitcast_dynamic-update-slice_fusion.7
  78.1 1.0 bitcast_dynamic-update-slice_fusion.6
  80.1 0.8 fusion.291
  80.9 1.2 bitcast_dynamic-update-slice_fusion.7
  87.2 1.0 bitcast_dynamic-update-slice_fusion.6
  90.1 1.2 bitcast_dynamic-update-slice_fusion.7
  96.4 1.0 bitcast_dynamic-update-slice_fusion.6
  99.2 1.2 bitcast_dynamic-update-slice_fusion.7
  105.5 1.0 bitcast_dynamic-update-slice_fusion.6
  108.3 1.2 bitcast_dynamic-update-slice_fusion.7
  114.6 1.0 bitcast_dynamic-update-slice_fusion.6
  117.5 1.2 bitcast_dynamic-update-slice_fusion.7
  119.1 26.7 %all-gather.5.cloned.1.call-done = bf16[32,128,128]{2,1,0:T(8,128)(2,1)} async-done(((bf16[8,128,128]{2,1,0:T(8,128)(2,1)}), bf16[32,128,128]{2,1,0:T(8,128)(2,1)}) %all-gather.5.cloned.1.call-update) | async-done | bytes 1048592 | tf_op jit(solution)/shard_map/all_gather | solution.py:27
  146.3 14.4 %while.64 = (s32[]{:T(128)}, f32[8,128]{1,0:T(8,128)S(1)}, f32[8,8,128]{2,1,0:T(8,128)S(1)}, f32[8,8,128,128]{3,2,1,0:T(8,128)}, s32[]{:T(128)}, /*index=5*/f32[]{:T(128)}) while((s32[]{:T(128)}, f32[8,128]{1,0:T(8,128)S(1)}, f32[8,8,128]{2,1,0:T(8,128)S(1)}, f32[8,8,128,128]{3,2,1,0:T(8,128)}, s32[]{:T(128)}, /*index=5*/f32[]{:T(128)}) %tuple.188), condition=%wide.region_26.27_spmd, body=%wide.region_24.26_spmd.sunk | while | flops 1574906 | bytes 553613 | solution.py:160
  146.3 1.6 fusion.296
  148.1 1.6 fusion.296
  149.9 1.6 fusion.296
  151.7 1.6 fusion.296
  153.5 1.6 fusion.296
  155.3 1.6 fusion.296
  157.1 1.6 fusion.296
  158.9 1.6 fusion.296
  161.9 5.0 %while.65 = (s32[]{:T(128)}, f32[8,128,128]{2,1,0:T(8,128)S(1)}, s32[]{:T(128)}, bf16[4,8,128,128]{3,2,1,0:T(8,128)(2,1)}, s32[]{:T(128)}, /*index=5*/s32[]{:T(128)}, s32[]{:T(128)}, s32[]{:T(128)}) while((s32[]{:T(128)}, f32[8,128,128]{2,1,0:T(8,128)S(1)}, s32[]{:T(128)}, bf16[4,8,128,128]{3,2,1,0:T(8,128)(2,1)}, s32[]{:T(128)}, ...), condition=%wide.region_37.38_spmd, body=%wide.region_35.37_spmd.sunk | while | flops 201588736 | bytes 2359495 | solution.py:34
  162.0 1.4 fusion.298
  163.6 1.4 fusion.298
  165.2 1.4 fusion.298
  167.3 17.6 %while.66 = (s32[]{:T(128)}, f32[8,128]{1,0:T(8,128)S(1)}, f32[8,8,128]{2,0,1:T(8,128)S(1)}, f32[8,8,128,128]{3,2,1,0:T(8,128)}, s32[]{:T(128)}, /*index=5*/s32[]{:T(128)}, f32[]{:T(128)}, s32[]{:T(128)}) while((s32[]{:T(128)}, f32[8,128]{1,0:T(8,128)S(1)}, f32[8,8,128]{2,0,1:T(8,128)S(1)}, f32[8,8,128,128]{3,2,1,0:T(8,128)}, s32[]{:T(128)}, ...), condition=%wide.region_42.43_spmd, body=%wide.region_40.42_spmd.sunk | while | flops 1574907 | bytes 553133 | solution.py:161
  167.3 2.0 fusion.301
  169.5 2.0 fusion.301
  171.7 2.0 fusion.301
  173.9 2.0 fusion.301
  176.1 2.0 fusion.301
  178.3 2.0 fusion.301
  180.6 2.0 fusion.301
  182.8 2.0 fusion.301
  192.7 0.9 fusion.149
  194.2 1.0 fusion.161
  195.8 1.0 fusion.159
  197.4 1.0 fusion.157
  199.0 1.0 fusion.155
  200.6 1.0 fusion.153
  202.2 1.0 fusion.151
  205.4 0.9 fusion.94
  (260 shorter events, 75.0 us)
Async XLA Ops:
  6.5 38.6 %copy-start = (bf16[8,768,128]{2,1,0:T(8,128)(2,1)S(1)}, bf16[8,768,128]{2,1,0:T(8,128)(2,1)}, u32[]{:S(2)}) copy-start(bf16[8,768,128]{2,1,0:T(8,128)(2,1)} %param.20) | copy-start | bytes 4718596
  6.5 11.0 %copy-start.1 = (f32[8,128,128]{2,1,0:T(8,128)S(1)}, f32[8,128,128]{2,1,0:T(8,128)}, u32[]{:S(2)}) copy-start(f32[8,128,128]{2,1,0:T(8,128)} %param.21) | copy-start | bytes 1572868
  6.5 139.3 %all-gather.5.cloned.1.call-start = ((), (), s32[]{:S(2)}) async-start(), calls=%async_computation | async-start | bytes 1310720 | tf_op jit(solution)/shard_map/all_gather | solution.py:27
  9.6 8.1 %collective-permute-start = (bf16[4,768]{1,0:T(4,128)(2,1)S(1)}, bf16[4,768]{1,0:T(4,128)(2,1)S(1)}, u32[]{:S(2)}, u32[]{:S(2)}) collective-permute-start(bf16[4,768]{1,0:T(4,128)(2,1)S(1)} %get-tuple-element.359), channel_id=1, source_target_pairs={{0,4},{4,8},{8,12},{1,5},{5,9},{9,13},{2,6},{6,10},{10,14},{3,7},{... | collective-permute-start | bytes 18440 | tf_op jit(solution)/shard_map/ppermute | solution.py:15
  14.5 5.5 %collective-permute-start.1 = (bf16[4,768]{1,0:T(4,128)(2,1)S(1)}, bf16[4,768]{1,0:T(4,128)(2,1)S(1)}, u32[]{:S(2)}, u32[]{:S(2)}) collective-permute-start(bf16[4,768]{1,0:T(4,128)(2,1)S(1)} %get-tuple-element.360), channel_id=1, source_target_pairs={{4,0},{8,4},{12,8},{5,1},{9,5},{13,9},{6,2},{10,6},{14,10},{7,3},{... | collective-permute-start | bytes 18440 | tf_op jit(solution)/shard_map/ppermute | solution.py:18
  28.3 5.4 %collective-permute-start.2 = (bf16[8,768]{1,0:T(8,128)(2,1)S(1)}, bf16[8,768]{1,0:T(8,128)(2,1)S(1)}, u32[]{:S(2)}, u32[]{:S(2)}) collective-permute-start(bf16[8,768]{1,0:T(8,128)(2,1)S(1)} %get-tuple-element.357), channel_id=1, source_target_pairs={{0,4},{4,8},{8,12},{1,5},{5,9},{9,13},{2,6},{6,10},{10,14},{3,7},{... | collective-permute-start | bytes 36872 | tf_op jit(solution)/shard_map/ppermute | solution.py:15
  31.8 5.6 %collective-permute-start.3 = (bf16[8,768]{1,0:T(8,128)(2,1)S(1)}, bf16[8,768]{1,0:T(8,128)(2,1)S(1)}, u32[]{:S(2)}, u32[]{:S(2)}) collective-permute-start(bf16[8,768]{1,0:T(8,128)(2,1)S(1)} %get-tuple-element.358), channel_id=1, source_target_pairs={{4,0},{8,4},{12,8},{5,1},{9,5},{13,9},{6,2},{10,6},{14,10},{7,3},{... | collective-permute-start | bytes 36872 | tf_op jit(solution)/shard_map/ppermute | solution.py:18
Sparse Core Ops, SparseCore 0:
  118.9 26.8 all-gather.4
